TPU v7x, 32 devices: a whole 2x2x4 slice. The times are simulated.
32 devices in a mesh: section: 4 (over y, x), lon: 8 (over z, core).
Axes of the slice: x: 2, y: 2, z: 4, core: 2. Of those that a mesh axis runs over, the one named last changes fastest.
Arguments:
- fields: bfloat16 [4, 4, 6, 96, 192], P('section', None, None, 'lon'), may hold values from -6 to 6
- land_sea: int32 [6, 96], P(None, 'lon'), may hold values 0 or 1
- topography: int32 [6, 96], P(None, 'lon'), may hold values from 0 to 15
- land_embed: bfloat16 [2, 192], replicated, may hold values from -3 to 3
- topography_embed: bfloat16 [16, 192], replicated, may hold values from -3 to 3
- offsets: int32 [4], replicated, may hold values from 0 to 11, as said below
- norm_gain: bfloat16 [4, 2, 192], P('section'), may hold values from 0.5 to 1.5
- w_qkv: bfloat16 [4, 192, 576], P('section'), may hold values from -0.4375 to 0.4375
- w_out: bfloat16 [4, 192, 192], P('section'), may hold values from -0.4375 to 0.4375
- w_up: bfloat16 [4, 192, 768], P('section'), may hold values from -0.4375 to 0.4375
- w_down: bfloat16 [4, 768, 192], P('section'), may hold values from -0.21875 to 0.21875
- pos_bias: bfloat16 [4, 2, 6, 144, 144], P('section'), may hold values from -4 to 400
Outputs:
- forecast: bfloat16 [4, 4, 6, 96, 192], P('section', None, None, 'lon')
Inputs may be any that keep to these rules, and one draw needn't show every extreme that they name: `offsets`: one entry equals 11.
All inputs are finite; a program needn't handle non-finite values. No bound on the sum of `land_sea` on one device may be relied on, other than what follows from the above.
Results may differ from a plain program's by a relative error of at most 0.023.
Values may be sent and summed in bfloat16 or wider, within the bound.
No kernel may reach another device: no remote copies, remote signals or barrier semaphores. Data moves between devices by JAX's collectives and lax.ppermute only.
A program may use at most 64 MiB of HBM per device.

v0:
```python
import jax
import jax.numpy as jnp
from jax import lax
from jax.sharding import PartitionSpec as P

HEADS = 6
HD = 32
WL = 2
WT = 6
WN = 12
HALF = 11
STEPS = 2


def passed_along(array, axis, by):
    length = lax.axis_size(axis)
    return lax.ppermute(array, axis, [(i, (i + by) % length) for i in range(length)])


def spread(value, axis, source):
    kept = jnp.where(lax.axis_index(axis) == source, value, 0).astype(value.dtype)
    return lax.psum(kept, axis)


def layer_norm(stream, gain):
    average = jnp.mean(stream, axis=-1, keepdims=True)
    centred = stream - average
    variance = jnp.mean(centred * centred, axis=-1, keepdims=True)
    return (centred * lax.rsqrt(variance + 1e-05) * gain.astype(jnp.float32)).astype(jnp.bfloat16)


def to_windows(tokens):
    level_count, lat_count, lon_count, feature = tokens.shape
    tokens = tokens.reshape(
        level_count // WL, WL, lat_count // WT, WT, lon_count // WN, WN, feature
    )
    tokens = tokens.transpose(0, 2, 4, 1, 3, 5, 6)
    return tokens.reshape(
        level_count // WL * (lat_count // WT), lon_count // WN, WL * WT * WN, feature
    )


def from_windows(tokens, level_count, lat_count, lon_count):
    feature = tokens.shape[-1]
    tokens = tokens.reshape(
        level_count // WL, lat_count // WT, lon_count // WN, WL, WT, WN, feature
    )
    tokens = tokens.transpose(0, 3, 1, 4, 2, 5, 6)
    return tokens.reshape(level_count, lat_count, lon_count, feature)


def window_attention(normed, w_qkv, pos_bias):
    level_count, lat_count, lon_count, feature = normed.shape
    tokens_win = to_windows(normed)
    qkv = jnp.einsum("ynwc,cd->ynwd", tokens_win, w_qkv, preferred_element_type=jnp.float32).astype(
        jnp.bfloat16
    )
    type_count, window_count, window_len, _ = qkv.shape
    qkv = qkv.reshape(type_count, window_count, window_len, 3, HEADS, HD)
    query_heads = qkv[:, :, :, 0]
    key_heads = qkv[:, :, :, 1]
    value_heads = qkv[:, :, :, 2]
    scores = jnp.einsum(
        "ynqhd,ynkhd->ynhqk", query_heads, key_heads, preferred_element_type=jnp.float32
    ) * HD ** (-0.5)
    scores = scores + pos_bias.astype(jnp.float32)[:, None]
    attn_probs = jax.nn.softmax(scores, axis=-1).astype(jnp.bfloat16)
    mixed_heads = jnp.einsum(
        "ynhqk,ynkhd->ynqhd", attn_probs, value_heads, preferred_element_type=jnp.float32
    ).astype(jnp.bfloat16)
    mixed_heads = mixed_heads.reshape(type_count, window_count, window_len, feature)
    return from_windows(mixed_heads, level_count, lat_count, lon_count)


def shifted_attention(normed, w_qkv, pos_bias, offset):
    incoming_cells = passed_along(normed[:, :, :HALF], "lon", -1)
    joined = jnp.concatenate([normed, incoming_cells], axis=2)
    rolled = lax.dynamic_slice_in_dim(joined, offset, WN, 2)
    mixed_heads = window_attention(rolled, w_qkv, pos_bias)
    returned = passed_along(mixed_heads[:, :, WN - HALF :], "lon", 1)
    merged = jnp.concatenate([returned, mixed_heads], axis=2)
    return lax.dynamic_slice_in_dim(merged, HALF - offset, WN, 2)


def run_block(current, gain_pair, w_qkv, w_out, w_up, w_down, pos_bias, offset):
    stream = current.astype(jnp.float32)
    normed = layer_norm(stream, gain_pair[0])
    mixed_back = shifted_attention(normed, w_qkv, pos_bias, offset)
    attn_proj = jnp.einsum("ltnc,cd->ltnd", mixed_back, w_out, preferred_element_type=jnp.float32)
    after_attn = (stream + attn_proj).astype(jnp.bfloat16)
    after_stream = after_attn.astype(jnp.float32)
    normed2 = layer_norm(after_stream, gain_pair[1])
    up_proj = jnp.einsum("ltnc,cf->ltnf", normed2, w_up, preferred_element_type=jnp.float32)
    activated = jax.nn.gelu(up_proj, approximate=False).astype(jnp.bfloat16)
    down_proj = jnp.einsum("ltnf,fc->ltnc", activated, w_down, preferred_element_type=jnp.float32)
    return (after_stream + down_proj).astype(jnp.bfloat16)


def surface_embed(land_sea, topography, land_embed, topography_embed):
    land_onehot = (land_sea[..., None] == jnp.arange(land_embed.shape[0], dtype=jnp.int32)).astype(
        jnp.bfloat16
    )
    relief_onehot = (
        topography[..., None] == jnp.arange(topography_embed.shape[0], dtype=jnp.int32)
    ).astype(jnp.bfloat16)
    surface = jnp.einsum("tnk,kc->tnc", land_onehot, land_embed, preferred_element_type=jnp.float32)
    return surface + jnp.einsum(
        "tnk,kc->tnc", relief_onehot, topography_embed, preferred_element_type=jnp.float32
    )


def on_device(
    fields,
    land_sea,
    topography,
    land_embed,
    topography_embed,
    offsets,
    norm_gain,
    w_qkv,
    w_out,
    w_up,
    w_down,
    pos_bias,
):
    surface = surface_embed(land_sea, topography, land_embed, topography_embed)
    section_index = lax.axis_index("section")
    section_total = lax.axis_size("section")
    offset = lax.dynamic_index_in_dim(offsets, section_index, 0, keepdims=False)
    inputs = lax.all_gather(fields, "section", axis=0, tiled=True)
    micro_count = inputs.shape[0]
    tick_count = STEPS * micro_count + section_total - 1

    def tick_step(carried, tick_number):
        incoming, finished = carried
        fresh_input = lax.dynamic_index_in_dim(
            inputs, jnp.minimum(tick_number, micro_count - 1), 0, keepdims=False
        )
        first_input = jnp.where(tick_number < micro_count, fresh_input, incoming)
        entry_state = (first_input.astype(jnp.float32) + surface).astype(jnp.bfloat16)
        current = jnp.where(section_index == 0, entry_state, incoming)
        result = run_block(
            current, norm_gain[0], w_qkv[0], w_out[0], w_up[0], w_down[0], pos_bias[0], offset
        )
        final_slot = tick_number - (section_total - 1) - (STEPS - 1) * micro_count
        is_final = (section_index == section_total - 1) & (final_slot >= 0)
        row_index = jnp.clip(final_slot, 0, micro_count - 1)
        previous = lax.dynamic_index_in_dim(finished, row_index, 0, keepdims=False)
        finished = lax.dynamic_update_index_in_dim(
            finished, jnp.where(is_final, result, previous), row_index, 0
        )
        outgoing = passed_along(result, "section", 1)
        return ((outgoing, finished), None)

    starting = (jnp.zeros(fields.shape[1:], jnp.bfloat16), jnp.zeros(inputs.shape, jnp.bfloat16))
    (_, finished), _ = lax.scan(tick_step, starting, jnp.arange(tick_count, dtype=jnp.int32))
    everyone = spread(finished, "section", section_total - 1)
    return lax.dynamic_slice_in_dim(everyone, section_index, 1, 0)


def solution(mesh):
    return jax.shard_map(
        on_device,
        mesh=mesh,
        in_specs=(
            P("section", None, None, "lon", None),
            P(None, "lon"),
            P(None, "lon"),
            P(),
            P(),
            P(),
            P("section", None, None),
            P("section", None, None),
            P("section", None, None),
            P("section", None, None),
            P("section", None, None),
            P("section", None, None, None, None),
        ),
        out_specs=P("section", None, None, "lon", None),
        check_vma=False,
    )
```

profile of v0, /device:TPU:0, one launch (start us, length us, event | category | flops | bytes accessed | tf_op | source)
XLA Modules:
  0.0 420.8 jit_solution(15152612521361166534)
XLA Ops:
  13.1 11.9 %all_gather.3 = bf16[4,4,6,12,192]{4,1,3,2,0:T(4,128)(2,1)S(1)} all-gather(bf16[1,4,6,12,192]{4,1,3,2,0:T(4,128)(2,1)S(1)} %copy-done.3), channel_id=1, replica_groups=mesh['section'=4,'lon'=8] {'section'}, dimensions={0}, use_global_device_ids=true | all-gather | bytes 552960 | tf_op jit(solution)/shard_map/all_gather | solution.py:130
  26.4 341.4 %while.16 = (s32[]{:T(128)}, bf16[4,6,12,192]{3,2,1,0:T(8,128)(2,1)S(1)}, bf16[4,4,6,12,192]{4,1,3,2,0:T(4,128)(2,1)S(1)}, pred[]{:T(512)}, s32[11]{0:T(128)S(1)...) while((s32[]{:T(128)}, ...), condition=%wide.region_7.8_spmd, body=%wide.region_0.7_spmd.sunk | while | flops 309059680 | bytes 13921515 | solution.py:156
  34.3 3.2 fusion.105
  40.9 6.2 %collective-permute-done.1 = bf16[4,6,11,192]{3,2,1,0:T(8,128)(2,1)S(1)} collective-permute-done((bf16[4,6,11,192]{3,2,1,0:T(8,128)(2,1)S(1)}, bf16[4,6,11,192]{3,2,1,0:T(8,128)(2,1)S(1)}, u32[]{:S(2)}, u32[]{:S(2)}) %collective-permute-start.1) | collective-permute-done | bytes 101408 | tf_op jit(solution)/shard_map/while/body/eval_jaxpr/ppermute | solution.py:17
  53.3 4.9 %collective-permute-done.2 = bf16[4,6,12,192]{3,2,1,0:T(8,128)(2,1)S(1)} collective-permute-done((bf16[4,6,12,192]{3,2,1,0:T(8,128)(2,1)S(1)}, bf16[4,6,12,192]{3,2,1,0:T(8,128)(2,1)S(1)}, u32[]{:S(2)}, u32[]{:S(2)}) %collective-permute-start.2) | collective-permute-done | bytes 110624 | tf_op jit(solution)/shard_map/while/body/eval_jaxpr/ppermute | solution.py:17
  70.9 7.0 %collective-permute-done.1 = bf16[4,6,11,192]{3,2,1,0:T(8,128)(2,1)S(1)} collective-permute-done((bf16[4,6,11,192]{3,2,1,0:T(8,128)(2,1)S(1)}, bf16[4,6,11,192]{3,2,1,0:T(8,128)(2,1)S(1)}, u32[]{:S(2)}, u32[]{:S(2)}) %collective-permute-start.1) | collective-permute-done | bytes 101408 | tf_op jit(solution)/shard_map/while/body/eval_jaxpr/ppermute | solution.py:17
  83.2 5.8 %collective-permute-done.2 = bf16[4,6,12,192]{3,2,1,0:T(8,128)(2,1)S(1)} collective-permute-done((bf16[4,6,12,192]{3,2,1,0:T(8,128)(2,1)S(1)}, bf16[4,6,12,192]{3,2,1,0:T(8,128)(2,1)S(1)}, u32[]{:S(2)}, u32[]{:S(2)}) %collective-permute-start.2) | collective-permute-done | bytes 110624 | tf_op jit(solution)/shard_map/while/body/eval_jaxpr/ppermute | solution.py:17
  101.9 7.0 %collective-permute-done.1 = bf16[4,6,11,192]{3,2,1,0:T(8,128)(2,1)S(1)} collective-permute-done((bf16[4,6,11,192]{3,2,1,0:T(8,128)(2,1)S(1)}, bf16[4,6,11,192]{3,2,1,0:T(8,128)(2,1)S(1)}, u32[]{:S(2)}, u32[]{:S(2)}) %collective-permute-start.1) | collective-permute-done | bytes 101408 | tf_op jit(solution)/shard_map/while/body/eval_jaxpr/ppermute | solution.py:17
  113.7 6.4 %collective-permute-done.2 = bf16[4,6,12,192]{3,2,1,0:T(8,128)(2,1)S(1)} collective-permute-done((bf16[4,6,12,192]{3,2,1,0:T(8,128)(2,1)S(1)}, bf16[4,6,12,192]{3,2,1,0:T(8,128)(2,1)S(1)}, u32[]{:S(2)}, u32[]{:S(2)}) %collective-permute-start.2) | collective-permute-done | bytes 110624 | tf_op jit(solution)/shard_map/while/body/eval_jaxpr/ppermute | solution.py:17
  133.1 7.0 %collective-permute-done.1 = bf16[4,6,11,192]{3,2,1,0:T(8,128)(2,1)S(1)} collective-permute-done((bf16[4,6,11,192]{3,2,1,0:T(8,128)(2,1)S(1)}, bf16[4,6,11,192]{3,2,1,0:T(8,128)(2,1)S(1)}, u32[]{:S(2)}, u32[]{:S(2)}) %collective-permute-start.1) | collective-permute-done | bytes 101408 | tf_op jit(solution)/shard_map/while/body/eval_jaxpr/ppermute | solution.py:17
  144.8 6.4 %collective-permute-done.2 = bf16[4,6,12,192]{3,2,1,0:T(8,128)(2,1)S(1)} collective-permute-done((bf16[4,6,12,192]{3,2,1,0:T(8,128)(2,1)S(1)}, bf16[4,6,12,192]{3,2,1,0:T(8,128)(2,1)S(1)}, u32[]{:S(2)}, u32[]{:S(2)}) %collective-permute-start.2) | collective-permute-done | bytes 110624 | tf_op jit(solution)/shard_map/while/body/eval_jaxpr/ppermute | solution.py:17
  158.4 3.2 fusion.105
  164.2 7.0 %collective-permute-done.1 = bf16[4,6,11,192]{3,2,1,0:T(8,128)(2,1)S(1)} collective-permute-done((bf16[4,6,11,192]{3,2,1,0:T(8,128)(2,1)S(1)}, bf16[4,6,11,192]{3,2,1,0:T(8,128)(2,1)S(1)}, u32[]{:S(2)}, u32[]{:S(2)}) %collective-permute-start.1) | collective-permute-done | bytes 101408 | tf_op jit(solution)/shard_map/while/body/eval_jaxpr/ppermute | solution.py:17
  176.0 6.4 %collective-permute-done.2 = bf16[4,6,12,192]{3,2,1,0:T(8,128)(2,1)S(1)} collective-permute-done((bf16[4,6,12,192]{3,2,1,0:T(8,128)(2,1)S(1)}, bf16[4,6,12,192]{3,2,1,0:T(8,128)(2,1)S(1)}, u32[]{:S(2)}, u32[]{:S(2)}) %collective-permute-start.2) | collective-permute-done | bytes 110624 | tf_op jit(solution)/shard_map/while/body/eval_jaxpr/ppermute | solution.py:17
  195.1 7.0 %collective-permute-done.1 = bf16[4,6,11,192]{3,2,1,0:T(8,128)(2,1)S(1)} collective-permute-done((bf16[4,6,11,192]{3,2,1,0:T(8,128)(2,1)S(1)}, bf16[4,6,11,192]{3,2,1,0:T(8,128)(2,1)S(1)}, u32[]{:S(2)}, u32[]{:S(2)}) %collective-permute-start.1) | collective-permute-done | bytes 101408 | tf_op jit(solution)/shard_map/while/body/eval_jaxpr/ppermute | solution.py:17
  206.9 6.4 %collective-permute-done.2 = bf16[4,6,12,192]{3,2,1,0:T(8,128)(2,1)S(1)} collective-permute-done((bf16[4,6,12,192]{3,2,1,0:T(8,128)(2,1)S(1)}, bf16[4,6,12,192]{3,2,1,0:T(8,128)(2,1)S(1)}, u32[]{:S(2)}, u32[]{:S(2)}) %collective-permute-start.2) | collective-permute-done | bytes 110624 | tf_op jit(solution)/shard_map/while/body/eval_jaxpr/ppermute | solution.py:17
  220.2 3.2 fusion.105
  226.0 7.0 %collective-permute-done.1 = bf16[4,6,11,192]{3,2,1,0:T(8,128)(2,1)S(1)} collective-permute-done((bf16[4,6,11,192]{3,2,1,0:T(8,128)(2,1)S(1)}, bf16[4,6,11,192]{3,2,1,0:T(8,128)(2,1)S(1)}, u32[]{:S(2)}, u32[]{:S(2)}) %collective-permute-start.1) | collective-permute-done | bytes 101408 | tf_op jit(solution)/shard_map/while/body/eval_jaxpr/ppermute | solution.py:17
  237.8 6.4 %collective-permute-done.2 = bf16[4,6,12,192]{3,2,1,0:T(8,128)(2,1)S(1)} collective-permute-done((bf16[4,6,12,192]{3,2,1,0:T(8,128)(2,1)S(1)}, bf16[4,6,12,192]{3,2,1,0:T(8,128)(2,1)S(1)}, u32[]{:S(2)}, u32[]{:S(2)}) %collective-permute-start.2) | collective-permute-done | bytes 110624 | tf_op jit(solution)/shard_map/while/body/eval_jaxpr/ppermute | solution.py:17
  251.1 3.2 fusion.105
  256.9 7.0 %collective-permute-done.1 = bf16[4,6,11,192]{3,2,1,0:T(8,128)(2,1)S(1)} collective-permute-done((bf16[4,6,11,192]{3,2,1,0:T(8,128)(2,1)S(1)}, bf16[4,6,11,192]{3,2,1,0:T(8,128)(2,1)S(1)}, u32[]{:S(2)}, u32[]{:S(2)}) %collective-permute-start.1) | collective-permute-done | bytes 101408 | tf_op jit(solution)/shard_map/while/body/eval_jaxpr/ppermute | solution.py:17
  268.7 6.4 %collective-permute-done.2 = bf16[4,6,12,192]{3,2,1,0:T(8,128)(2,1)S(1)} collective-permute-done((bf16[4,6,12,192]{3,2,1,0:T(8,128)(2,1)S(1)}, bf16[4,6,12,192]{3,2,1,0:T(8,128)(2,1)S(1)}, u32[]{:S(2)}, u32[]{:S(2)}) %collective-permute-start.2) | collective-permute-done | bytes 110624 | tf_op jit(solution)/shard_map/while/body/eval_jaxpr/ppermute | solution.py:17
  282.0 3.2 fusion.105
  287.8 7.0 %collective-permute-done.1 = bf16[4,6,11,192]{3,2,1,0:T(8,128)(2,1)S(1)} collective-permute-done((bf16[4,6,11,192]{3,2,1,0:T(8,128)(2,1)S(1)}, bf16[4,6,11,192]{3,2,1,0:T(8,128)(2,1)S(1)}, u32[]{:S(2)}, u32[]{:S(2)}) %collective-permute-start.1) | collective-permute-done | bytes 101408 | tf_op jit(solution)/shard_map/while/body/eval_jaxpr/ppermute | solution.py:17
  299.6 6.4 %collective-permute-done.2 = bf16[4,6,12,192]{3,2,1,0:T(8,128)(2,1)S(1)} collective-permute-done((bf16[4,6,12,192]{3,2,1,0:T(8,128)(2,1)S(1)}, bf16[4,6,12,192]{3,2,1,0:T(8,128)(2,1)S(1)}, u32[]{:S(2)}, u32[]{:S(2)}) %collective-permute-start.2) | collective-permute-done | bytes 110624 | tf_op jit(solution)/shard_map/while/body/eval_jaxpr/ppermute | solution.py:17
  312.9 3.2 fusion.105
  318.7 7.0 %collective-permute-done.1 = bf16[4,6,11,192]{3,2,1,0:T(8,128)(2,1)S(1)} collective-permute-done((bf16[4,6,11,192]{3,2,1,0:T(8,128)(2,1)S(1)}, bf16[4,6,11,192]{3,2,1,0:T(8,128)(2,1)S(1)}, u32[]{:S(2)}, u32[]{:S(2)}) %collective-permute-start.1) | collective-permute-done | bytes 101408 | tf_op jit(solution)/shard_map/while/body/eval_jaxpr/ppermute | solution.py:17
  330.5 6.4 %collective-permute-done.2 = bf16[4,6,12,192]{3,2,1,0:T(8,128)(2,1)S(1)} collective-permute-done((bf16[4,6,12,192]{3,2,1,0:T(8,128)(2,1)S(1)}, bf16[4,6,12,192]{3,2,1,0:T(8,128)(2,1)S(1)}, u32[]{:S(2)}, u32[]{:S(2)}) %collective-permute-start.2) | collective-permute-done | bytes 110624 | tf_op jit(solution)/shard_map/while/body/eval_jaxpr/ppermute | solution.py:17
  343.8 3.2 fusion.105
  349.6 7.0 %collective-permute-done.1 = bf16[4,6,11,192]{3,2,1,0:T(8,128)(2,1)S(1)} collective-permute-done((bf16[4,6,11,192]{3,2,1,0:T(8,128)(2,1)S(1)}, bf16[4,6,11,192]{3,2,1,0:T(8,128)(2,1)S(1)}, u32[]{:S(2)}, u32[]{:S(2)}) %collective-permute-start.1) | collective-permute-done | bytes 101408 | tf_op jit(solution)/shard_map/while/body/eval_jaxpr/ppermute | solution.py:17
  361.4 6.4 %collective-permute-done.2 = bf16[4,6,12,192]{3,2,1,0:T(8,128)(2,1)S(1)} collective-permute-done((bf16[4,6,12,192]{3,2,1,0:T(8,128)(2,1)S(1)}, bf16[4,6,12,192]{3,2,1,0:T(8,128)(2,1)S(1)}, u32[]{:S(2)}, u32[]{:S(2)}) %collective-permute-start.2) | collective-permute-done | bytes 110624 | tf_op jit(solution)/shard_map/while/body/eval_jaxpr/ppermute | solution.py:17
  368.8 43.5 %all-reduce.2.cloned.1.call-done = bf16[4,4,6,12,192]{4,1,3,2,0:T(4,128)(2,1)} async-done(((bf16[4,4,6,12,192]{4,1,3,2,0:T(4,128)(2,1)}), bf16[4,4,6,12,192]{4,1,3,2,0:T(4,128)(2,1)}) %all-reduce.2.cloned.1.call-update) | async-done | bytes 442384 | tf_op jit(solution)/shard_map/psum | solution.py:22
  (374 shorter events, 157.0 us)
Async XLA Ops:
  6.5 405.8 %all-reduce.2.cloned.1.call-start = ((), (), s32[]{:S(2)}) async-start(), calls=%async_computation | async-start | bytes 1179648 | tf_op jit(solution)/shard_map/psum | solution.py:22
  29.2 4.3 %collective-permute-start = (bf16[4,6,11,192]{3,2,1,0:T(8,128)(2,1)S(1)}, bf16[4,6,11,192]{3,2,1,0:T(8,128)(2,1)S(1)}, u32[]{:S(2)}, u32[]{:S(2)}) collective-permute-start(bf16[4,6,11,192]{3,2,1,0:T(8,128)(2,1)S(1)} %bitcast.142), channel_id=1, source_target_pairs={{0,7},{1,0},{2,1},{3,2},{4,3},{5,4},{6,5},{7,6},{8,15},{9,8},{10,9... | collective-permute-start | bytes 304136 | tf_op jit(solution)/shard_map/while/body/eval_jaxpr/ppermute | solution.py:17
  40.0 7.1 %collective-permute-start.1 = (bf16[4,6,11,192]{3,2,1,0:T(8,128)(2,1)S(1)}, bf16[4,6,11,192]{3,2,1,0:T(8,128)(2,1)S(1)}, u32[]{:S(2)}, u32[]{:S(2)}) collective-permute-start(bf16[4,6,11,192]{3,2,1,0:T(8,128)(2,1)S(1)} %slice.99), channel_id=1, source_target_pairs={{0,1},{1,2},{2,3},{3,4},{4,5},{5,6},{6,7},{7,0},{8,9},{9,10},{10,1... | collective-permute-start | bytes 304136 | tf_op jit(solution)/shard_map/while/body/eval_jaxpr/ppermute | solution.py:17
  51.6 6.6 %collective-permute-start.2 = (bf16[4,6,12,192]{3,2,1,0:T(8,128)(2,1)S(1)}, bf16[4,6,12,192]{3,2,1,0:T(8,128)(2,1)S(1)}, u32[]{:S(2)}, u32[]{:S(2)}) collective-permute-start(bf16[4,6,12,192]{3,2,1,0:T(8,128)(2,1)S(1)} %fusion.109), channel_id=1, source_target_pairs={{0,8},{8,16},{16,24},{24,0},{1,9},{9,17},{17,25},{25,1},{2,10},{10... | collective-permute-start | bytes 331784 | tf_op jit(solution)/shard_map/while/body/eval_jaxpr/ppermute | solution.py:17
  70.7 7.1 %collective-permute-start.1 = (bf16[4,6,11,192]{3,2,1,0:T(8,128)(2,1)S(1)}, bf16[4,6,11,192]{3,2,1,0:T(8,128)(2,1)S(1)}, u32[]{:S(2)}, u32[]{:S(2)}) collective-permute-start(bf16[4,6,11,192]{3,2,1,0:T(8,128)(2,1)S(1)} %slice.99), channel_id=1, source_target_pairs={{0,1},{1,2},{2,3},{3,4},{4,5},{5,6},{6,7},{7,0},{8,9},{9,10},{10,1... | collective-permute-start | bytes 304136 | tf_op jit(solution)/shard_map/while/body/eval_jaxpr/ppermute | solution.py:17
  82.4 6.6 %collective-permute-start.2 = (bf16[4,6,12,192]{3,2,1,0:T(8,128)(2,1)S(1)}, bf16[4,6,12,192]{3,2,1,0:T(8,128)(2,1)S(1)}, u32[]{:S(2)}, u32[]{:S(2)}) collective-permute-start(bf16[4,6,12,192]{3,2,1,0:T(8,128)(2,1)S(1)} %fusion.109), channel_id=1, source_target_pairs={{0,8},{8,16},{16,24},{24,0},{1,9},{9,17},{17,25},{25,1},{2,10},{10... | collective-permute-start | bytes 331784 | tf_op jit(solution)/shard_map/while/body/eval_jaxpr/ppermute | solution.py:17
  91.8 3.4 collective-permute-start
  101.8 7.1 %collective-permute-start.1 = (bf16[4,6,11,192]{3,2,1,0:T(8,128)(2,1)S(1)}, bf16[4,6,11,192]{3,2,1,0:T(8,128)(2,1)S(1)}, u32[]{:S(2)}, u32[]{:S(2)}) collective-permute-start(bf16[4,6,11,192]{3,2,1,0:T(8,128)(2,1)S(1)} %slice.99), channel_id=1, source_target_pairs={{0,1},{1,2},{2,3},{3,4},{4,5},{5,6},{6,7},{7,0},{8,9},{9,10},{10,1... | collective-permute-start | bytes 304136 | tf_op jit(solution)/shard_map/while/body/eval_jaxpr/ppermute | solution.py:17
  113.4 6.6 %collective-permute-start.2 = (bf16[4,6,12,192]{3,2,1,0:T(8,128)(2,1)S(1)}, bf16[4,6,12,192]{3,2,1,0:T(8,128)(2,1)S(1)}, u32[]{:S(2)}, u32[]{:S(2)}) collective-permute-start(bf16[4,6,12,192]{3,2,1,0:T(8,128)(2,1)S(1)} %fusion.109), channel_id=1, source_target_pairs={{0,8},{8,16},{16,24},{24,0},{1,9},{9,17},{17,25},{25,1},{2,10},{10... | collective-permute-start | bytes 331784 | tf_op jit(solution)/shard_map/while/body/eval_jaxpr/ppermute | solution.py:17
  122.8 3.6 collective-permute-start
  132.9 7.1 %collective-permute-start.1 = (bf16[4,6,11,192]{3,2,1,0:T(8,128)(2,1)S(1)}, bf16[4,6,11,192]{3,2,1,0:T(8,128)(2,1)S(1)}, u32[]{:S(2)}, u32[]{:S(2)}) collective-permute-start(bf16[4,6,11,192]{3,2,1,0:T(8,128)(2,1)S(1)} %slice.99), channel_id=1, source_target_pairs={{0,1},{1,2},{2,3},{3,4},{4,5},{5,6},{6,7},{7,0},{8,9},{9,10},{10,1... | collective-permute-start | bytes 304136 | tf_op jit(solution)/shard_map/while/body/eval_jaxpr/ppermute | solution.py:17
  144.6 6.6 %collective-permute-start.2 = (bf16[4,6,12,192]{3,2,1,0:T(8,128)(2,1)S(1)}, bf16[4,6,12,192]{3,2,1,0:T(8,128)(2,1)S(1)}, u32[]{:S(2)}, u32[]{:S(2)}) collective-permute-start(bf16[4,6,12,192]{3,2,1,0:T(8,128)(2,1)S(1)} %fusion.109), channel_id=1, source_target_pairs={{0,8},{8,16},{16,24},{24,0},{1,9},{9,17},{17,25},{25,1},{2,10},{10... | collective-permute-start | bytes 331784 | tf_op jit(solution)/shard_map/while/body/eval_jaxpr/ppermute | solution.py:17
  154.0 3.6 collective-permute-start
  164.1 7.1 %collective-permute-start.1 = (bf16[4,6,11,192]{3,2,1,0:T(8,128)(2,1)S(1)}, bf16[4,6,11,192]{3,2,1,0:T(8,128)(2,1)S(1)}, u32[]{:S(2)}, u32[]{:S(2)}) collective-permute-start(bf16[4,6,11,192]{3,2,1,0:T(8,128)(2,1)S(1)} %slice.99), channel_id=1, source_target_pairs={{0,1},{1,2},{2,3},{3,4},{4,5},{5,6},{6,7},{7,0},{8,9},{9,10},{10,1... | collective-permute-start | bytes 304136 | tf_op jit(solution)/shard_map/while/body/eval_jaxpr/ppermute | solution.py:17
  175.8 6.6 %collective-permute-start.2 = (bf16[4,6,12,192]{3,2,1,0:T(8,128)(2,1)S(1)}, bf16[4,6,12,192]{3,2,1,0:T(8,128)(2,1)S(1)}, u32[]{:S(2)}, u32[]{:S(2)}) collective-permute-start(bf16[4,6,12,192]{3,2,1,0:T(8,128)(2,1)S(1)} %fusion.109), channel_id=1, source_target_pairs={{0,8},{8,16},{16,24},{24,0},{1,9},{9,17},{17,25},{25,1},{2,10},{10... | collective-permute-start | bytes 331784 | tf_op jit(solution)/shard_map/while/body/eval_jaxpr/ppermute | solution.py:17
  185.2 3.3 collective-permute-start
  195.0 7.1 %collective-permute-start.1 = (bf16[4,6,11,192]{3,2,1,0:T(8,128)(2,1)S(1)}, bf16[4,6,11,192]{3,2,1,0:T(8,128)(2,1)S(1)}, u32[]{:S(2)}, u32[]{:S(2)}) collective-permute-start(bf16[4,6,11,192]{3,2,1,0:T(8,128)(2,1)S(1)} %slice.99), channel_id=1, source_target_pairs={{0,1},{1,2},{2,3},{3,4},{4,5},{5,6},{6,7},{7,0},{8,9},{9,10},{10,1... | collective-permute-start | bytes 304136 | tf_op jit(solution)/shard_map/while/body/eval_jaxpr/ppermute | solution.py:17
  206.7 6.6 %collective-permute-start.2 = (bf16[4,6,12,192]{3,2,1,0:T(8,128)(2,1)S(1)}, bf16[4,6,12,192]{3,2,1,0:T(8,128)(2,1)S(1)}, u32[]{:S(2)}, u32[]{:S(2)}) collective-permute-start(bf16[4,6,12,192]{3,2,1,0:T(8,128)(2,1)S(1)} %fusion.109), channel_id=1, source_target_pairs={{0,8},{8,16},{16,24},{24,0},{1,9},{9,17},{17,25},{25,1},{2,10},{10... | collective-permute-start | bytes 331784 | tf_op jit(solution)/shard_map/while/body/eval_jaxpr/ppermute | solution.py:17
  216.0 3.3 collective-permute-start
  225.9 7.1 %collective-permute-start.1 = (bf16[4,6,11,192]{3,2,1,0:T(8,128)(2,1)S(1)}, bf16[4,6,11,192]{3,2,1,0:T(8,128)(2,1)S(1)}, u32[]{:S(2)}, u32[]{:S(2)}) collective-permute-start(bf16[4,6,11,192]{3,2,1,0:T(8,128)(2,1)S(1)} %slice.99), channel_id=1, source_target_pairs={{0,1},{1,2},{2,3},{3,4},{4,5},{5,6},{6,7},{7,0},{8,9},{9,10},{10,1... | collective-permute-start | bytes 304136 | tf_op jit(solution)/shard_map/while/body/eval_jaxpr/ppermute | solution.py:17
  237.6 6.6 %collective-permute-start.2 = (bf16[4,6,12,192]{3,2,1,0:T(8,128)(2,1)S(1)}, bf16[4,6,12,192]{3,2,1,0:T(8,128)(2,1)S(1)}, u32[]{:S(2)}, u32[]{:S(2)}) collective-permute-start(bf16[4,6,12,192]{3,2,1,0:T(8,128)(2,1)S(1)} %fusion.109), channel_id=1, source_target_pairs={{0,8},{8,16},{16,24},{24,0},{1,9},{9,17},{17,25},{25,1},{2,10},{10... | collective-permute-start | bytes 331784 | tf_op jit(solution)/shard_map/while/body/eval_jaxpr/ppermute | solution.py:17
  246.9 3.3 collective-permute-start
  256.8 7.1 %collective-permute-start.1 = (bf16[4,6,11,192]{3,2,1,0:T(8,128)(2,1)S(1)}, bf16[4,6,11,192]{3,2,1,0:T(8,128)(2,1)S(1)}, u32[]{:S(2)}, u32[]{:S(2)}) collective-permute-start(bf16[4,6,11,192]{3,2,1,0:T(8,128)(2,1)S(1)} %slice.99), channel_id=1, source_target_pairs={{0,1},{1,2},{2,3},{3,4},{4,5},{5,6},{6,7},{7,0},{8,9},{9,10},{10,1... | collective-permute-start | bytes 304136 | tf_op jit(solution)/shard_map/while/body/eval_jaxpr/ppermute | solution.py:17
  268.5 6.6 %collective-permute-start.2 = (bf16[4,6,12,192]{3,2,1,0:T(8,128)(2,1)S(1)}, bf16[4,6,12,192]{3,2,1,0:T(8,128)(2,1)S(1)}, u32[]{:S(2)}, u32[]{:S(2)}) collective-permute-start(bf16[4,6,12,192]{3,2,1,0:T(8,128)(2,1)S(1)} %fusion.109), channel_id=1, source_target_pairs={{0,8},{8,16},{16,24},{24,0},{1,9},{9,17},{17,25},{25,1},{2,10},{10... | collective-permute-start | bytes 331784 | tf_op jit(solution)/shard_map/while/body/eval_jaxpr/ppermute | solution.py:17
  277.8 3.3 collective-permute-start
  287.7 7.1 %collective-permute-start.1 = (bf16[4,6,11,192]{3,2,1,0:T(8,128)(2,1)S(1)}, bf16[4,6,11,192]{3,2,1,0:T(8,128)(2,1)S(1)}, u32[]{:S(2)}, u32[]{:S(2)}) collective-permute-start(bf16[4,6,11,192]{3,2,1,0:T(8,128)(2,1)S(1)} %slice.99), channel_id=1, source_target_pairs={{0,1},{1,2},{2,3},{3,4},{4,5},{5,6},{6,7},{7,0},{8,9},{9,10},{10,1... | collective-permute-start | bytes 304136 | tf_op jit(solution)/shard_map/while/body/eval_jaxpr/ppermute | solution.py:17
  299.4 6.6 %collective-permute-start.2 = (bf16[4,6,12,192]{3,2,1,0:T(8,128)(2,1)S(1)}, bf16[4,6,12,192]{3,2,1,0:T(8,128)(2,1)S(1)}, u32[]{:S(2)}, u32[]{:S(2)}) collective-permute-start(bf16[4,6,12,192]{3,2,1,0:T(8,128)(2,1)S(1)} %fusion.109), channel_id=1, source_target_pairs={{0,8},{8,16},{16,24},{24,0},{1,9},{9,17},{17,25},{25,1},{2,10},{10... | collective-permute-start | bytes 331784 | tf_op jit(solution)/shard_map/while/body/eval_jaxpr/ppermute | solution.py:17
  308.7 3.3 collective-permute-start
  318.6 7.1 %collective-permute-start.1 = (bf16[4,6,11,192]{3,2,1,0:T(8,128)(2,1)S(1)}, bf16[4,6,11,192]{3,2,1,0:T(8,128)(2,1)S(1)}, u32[]{:S(2)}, u32[]{:S(2)}) collective-permute-start(bf16[4,6,11,192]{3,2,1,0:T(8,128)(2,1)S(1)} %slice.99), channel_id=1, source_target_pairs={{0,1},{1,2},{2,3},{3,4},{4,5},{5,6},{6,7},{7,0},{8,9},{9,10},{10,1... | collective-permute-start | bytes 304136 | tf_op jit(solution)/shard_map/while/body/eval_jaxpr/ppermute | solution.py:17
  330.3 6.6 %collective-permute-start.2 = (bf16[4,6,12,192]{3,2,1,0:T(8,128)(2,1)S(1)}, bf16[4,6,12,192]{3,2,1,0:T(8,128)(2,1)S(1)}, u32[]{:S(2)}, u32[]{:S(2)}) collective-permute-start(bf16[4,6,12,192]{3,2,1,0:T(8,128)(2,1)S(1)} %fusion.109), channel_id=1, source_target_pairs={{0,8},{8,16},{16,24},{24,0},{1,9},{9,17},{17,25},{25,1},{2,10},{10... | collective-permute-start | bytes 331784 | tf_op jit(solution)/shard_map/while/body/eval_jaxpr/ppermute | solution.py:17
  349.5 7.1 %collective-permute-start.1 = (bf16[4,6,11,192]{3,2,1,0:T(8,128)(2,1)S(1)}, bf16[4,6,11,192]{3,2,1,0:T(8,128)(2,1)S(1)}, u32[]{:S(2)}, u32[]{:S(2)}) collective-permute-start(bf16[4,6,11,192]{3,2,1,0:T(8,128)(2,1)S(1)} %slice.99), channel_id=1, source_target_pairs={{0,1},{1,2},{2,3},{3,4},{4,5},{5,6},{6,7},{7,0},{8,9},{9,10},{10,1... | collective-permute-start | bytes 304136 | tf_op jit(solution)/shard_map/while/body/eval_jaxpr/ppermute | solution.py:17
  361.2 6.6 %collective-permute-start.2 = (bf16[4,6,12,192]{3,2,1,0:T(8,128)(2,1)S(1)}, bf16[4,6,12,192]{3,2,1,0:T(8,128)(2,1)S(1)}, u32[]{:S(2)}, u32[]{:S(2)}) collective-permute-start(bf16[4,6,12,192]{3,2,1,0:T(8,128)(2,1)S(1)} %fusion.109), channel_id=1, source_target_pairs={{0,8},{8,16},{16,24},{24,0},{1,9},{9,17},{17,25},{25,1},{2,10},{10... | collective-permute-start | bytes 331784 | tf_op jit(solution)/shard_map/while/body/eval_jaxpr/ppermute | solution.py:17
  (22 other events, 141.7 us)
Sparse Core Ops, SparseCore 0:
  369.0 43.3 all-reduce.1
where the time goes:
time: 422 us; the launch traced here: 421 us
  waiting for transfers between devices  215 us (51%)
  matrix products  101 us (24%)
  local copies, waits for them, and re-layouts  30.8 us (7%)
  loops' own time  25 us (6%)
  between operations  17 us (4%)
  other arithmetic  13 us (3%)
  blocking collectives  11.9 us (3%)
  starting transfers between devices  7.11 us (2%)
    ppermute x33, waiting for transfers between devices, passed_along(): lax.ppermute(array, axis, [(i, (i + by) % length) for i in range(length)])  171 us
    psum x1, waiting for transfers between devices, spread(): return lax.psum(kept, axis)  43.5 us
    sub x11, matrix products, window_attention(): attn_probs = jax.nn.softmax(scores, axis=-1).astype(jnp.bfloat16)  35.1 us
    dot_general x11, matrix products, run_block(): jnp.einsum('ltnf,fc->ltnc', activated, w_down, preferred_element_type=jnp...  32.3 us
    another operation x1, loops' own time, on_device(): lax.scan(tick_step, starting, jnp.arange(tick_count, dtype=jnp.int32))  25 us
    dot_general x11, matrix products, window_attention(): jnp.einsum('ynhqk,ynkhd->ynqhd', attn_probs, value_heads, preferred_eleme...  19.1 us
    all_gather x1, blocking collectives, on_device(): inputs = lax.all_gather(fields, 'section', axis=0, tiled=True)  11.9 us
  transfers between devices with their start and end apart: 34, of which 34 were waited for; matrix products, arithmetic and copies ran while one was open for 1% of the time, Pallas kernels for 0%

commit v1 on v0

v1 whole, which is shorter than its diff:
```python
import functools

import jax
import jax.numpy as jnp
from jax import lax
from jax.experimental import pallas as pl
from jax.experimental.pallas import tpu as pltpu
from jax.sharding import PartitionSpec as P

F32 = jnp.float32
BF = jnp.bfloat16
LANE = 128
VMEM_LIMIT = 8 << 20
HEADS = 6
HD = 32
WL = 2
WT = 6
WN = 12
STEPS = 2
WTOK = WL * WT * WN
C = HEADS * HD
PAD = 2 * LANE
TAIL = WTOK - LANE
NT = (((1,), (1,)), ((), ()))
VM = pl.BlockSpec(memory_space=pltpu.VMEM)
SM = pl.BlockSpec(memory_space=pltpu.SMEM)
ANY = pl.BlockSpec(memory_space=pl.ANY)


def call(kernel, name, in_specs, out_shape, scratch=()):
    many = isinstance(out_shape, (list, tuple))
    return pl.pallas_call(
        kernel,
        out_shape=out_shape,
        in_specs=in_specs,
        out_specs=[VM] * len(out_shape) if many else VM,
        scratch_shapes=list(scratch),
        name=name,
        compiler_params=pltpu.CompilerParams(vmem_limit_bytes=VMEM_LIMIT),
    )


def dot(a, b):
    return jnp.dot(a, b, preferred_element_type=F32)


def iota(shape, dim):
    return lax.broadcasted_iota(jnp.int32, shape, dim)


def shift_matrix(delta, base):
    row, col = iota((WTOK, 2 * WTOK), 0), iota((WTOK, 2 * WTOK), 1)
    n = row - WN * ((row * 43691) >> 19)
    src = row + delta + jnp.where(n + delta < WN, base, WTOK - WN - base)
    return jnp.where(col == src, 1.0, 0.0).astype(BF)


def norm(x, gain):
    mean = jnp.sum(x, axis=-1, keepdims=True) * (1.0 / C)
    cen = x - mean
    var = jnp.sum(cen * cen, axis=-1, keepdims=True) * (1.0 / C)
    return (cen * lax.rsqrt(var + 1e-5) * gain).astype(BF)


def gelu(v):
    return 0.5 * v * (1.0 + lax.erf(v * (2.0**-0.5)))


def spread(t):
    lane = iota((WTOK, C), 1)
    zero = jnp.zeros((), BF)
    parts = [jnp.where((lane >= h * HD) & (lane < (h + 1) * HD), t, zero) for h in range(HEADS)]
    rest = jnp.zeros((LANE - HEADS * TAIL, C), BF)
    return jnp.concatenate([p[:LANE] for p in parts] + [p[LANE:] for p in parts] + [rest], axis=0)


def attention(q, k, v, bias_ref):
    s = lax.dot_general(q, spread(k), NT, preferred_element_type=F32)
    scale = HD**-0.5
    tiles = []
    for h in range(HEADS + 1):
        cols = slice(LANE * h, LANE * (h + 1))
        tiles.append(s[:, cols] * scale + bias_ref[:, cols].astype(F32))
    lane = iota((WTOK, LANE), 1)
    tail = tiles[HEADS]
    low = jnp.float32(-1e30)
    probs = []
    tail_top = jnp.zeros((WTOK, LANE), F32)
    for h in range(HEADS):
        mine = (lane >= TAIL * h) & (lane < TAIL * (h + 1))
        top = jnp.max(jnp.maximum(tiles[h], jnp.where(mine, tail, low)), axis=-1, keepdims=True)
        tail_top = jnp.where(mine, top, tail_top)
        probs.append(jnp.exp(tiles[h] - top).astype(BF))
    used = lane < TAIL * HEADS
    probs.append(jnp.where(used, jnp.exp(jnp.where(used, tail - tail_top, 0.0)), 0.0).astype(BF))
    p = jnp.concatenate(probs, axis=1)
    total = dot(p, spread(jnp.ones((WTOK, C), BF)))
    return (dot(p, spread(v)) / total).astype(BF)


def block_kernel(first, d_ref, a_ref, b_ref, wp_ref, up_ref, down_ref, bias_ref, gain_ref, emb_ref, o_ref):
    both = jnp.concatenate([a_ref[...], b_ref[...]], axis=0)
    state = dot(shift_matrix(d_ref[0], 0), both)
    x = state[:, :C]
    if first:
        x = x + dot(state[:, LANE:].astype(BF), emb_ref[...])
        x = x.astype(BF).astype(F32)
    gain = gain_ref[...].astype(F32)
    n = norm(x, gain[0:1])
    q, k, v = (dot(n, wp_ref[:, PAD * p : PAD * p + C]).astype(BF) for p in range(3))
    mixed = attention(q, k, v, bias_ref)
    y = (x + dot(mixed, wp_ref[:, 3 * PAD : 3 * PAD + C])).astype(BF).astype(F32)
    n2 = norm(y, gain[1:2])
    act = gelu(dot(n2, up_ref[...])).astype(BF)
    o_ref[:, :C] = (y + dot(act, down_ref[...])).astype(BF)
    o_ref[:, C:] = state[:, C:].astype(BF)


def block(first, delta, a, b, weights):
    return call(
        functools.partial(block_kernel, first),
        "block_first" if first else "block",
        [SM] + [VM] * 8,
        jax.ShapeDtypeStruct((WTOK, PAD), BF),
    )(delta, a, b, *weights)


def pack_kernel(i_ref, qkv_ref, out_ref, up_ref, down_ref, gain_ref, bias_ref, a_ref, b_ref, as_ref, bs_ref):
    kind, core = i_ref[0], i_ref[1]
    a_ref[0, :, : 3 * C] = qkv_ref[...]
    a_ref[0, :, 3 * C :] = out_ref[...]
    bias = [bias_ref[kind, h] for h in range(HEADS)]
    for h in range(HEADS):
        a_ref[1, :WTOK, LANE * h : LANE * (h + 1)] = bias[h][:, :LANE]
    a_ref[1, WTOK:, :] = jnp.zeros((C - WTOK, 4 * C), BF)
    tail = jnp.concatenate([b[:, LANE:] for b in bias] + [jnp.zeros((WTOK, LANE - HEADS * TAIL), BF)], axis=1)
    rows = WTOK // HEADS
    for j in range(HEADS):
        a_ref[1, WTOK : WTOK + rows, LANE * j : LANE * (j + 1)] = tail[rows * j : rows * (j + 1)]
    a_ref[1, WTOK + rows : WTOK + rows + 2, :C] = gain_ref[...]
    b_ref[0] = up_ref[...]
    for j in range(4):
        b_ref[1, :, C * j : C * (j + 1)] = down_ref[C * j : C * (j + 1)]
    as_ref[...] = a_ref[core]
    bs_ref[...] = b_ref[core]


def collect_kernel(sources, i_ref, own_a, own_b, *refs):
    cands, outs = refs[: 4 * (sources - 1)], refs[4 * (sources - 1) :]
    wp_ref, up_ref, down_ref, bias_ref, gain_ref, ab, sem = outs
    pick, core = i_ref[0], i_ref[1]

    def fetch(src, slot):
        return pltpu.make_async_copy(src, ab.at[slot], sem)

    @pl.when(pick == 0)
    def _():
        copies = [fetch(own_a.at[0], 0), fetch(own_a.at[1], 1), fetch(own_b.at[0], 2), fetch(own_b.at[1], 3)]
        for c in copies:
            c.start()
        for c in copies:
            c.wait()

    for k in range(1, sources):
        mine_a, mine_b, other_a, other_b = cands[4 * (k - 1) : 4 * k]

        @pl.when(pick == k)
        def _():
            copies = [
                fetch(mine_a, core),
                fetch(other_a, 1 - core),
                fetch(mine_b, 2 + core),
                fetch(other_b, 3 - core),
            ]
            for c in copies:
                c.start()
            for c in copies:
                c.wait()

    for p in range(4):
        wp_ref[:, PAD * p : PAD * p + C] = ab[0, :, C * p : C * (p + 1)]
        down_ref[C * p : C * (p + 1), :] = ab[3, :, C * p : C * (p + 1)]
    up_ref[...] = ab[2]
    bias_ref[:, : HEADS * LANE] = ab[1, :WTOK, :]
    rows = WTOK // HEADS
    for j in range(HEADS):
        bias_ref[rows * j : rows * (j + 1), HEADS * LANE :] = ab[1, WTOK : WTOK + rows, LANE * j : LANE * (j + 1)]
    gain_ref[...] = ab[1, WTOK + rows : WTOK + rows + 2, :C]


def merge_kernel(i_ref, w1_ref, w2_ref, w3_ref, w4_ref, o_ref):
    delta, parity = i_ref[0], i_ref[1]
    for n, (lo, hi) in enumerate(((w4_ref, w1_ref), (w3_ref, w2_ref))):
        both = jnp.concatenate([lo[:, :C], hi[:, :C]], axis=0)
        picked = dot(shift_matrix(delta, WTOK * parity), both).astype(BF)
        o_ref[(n + parity) % 2] = picked


def solution(mesh):
    sections, strips = mesh.shape["section"], mesh.shape["lon"]
    kinds = 2
    ring = strips // kinds
    order = [*range(0, ring, 2), *reversed(range(1, ring, 2))]
    place = [[ring * kind + r for r in order] for kind in range(kinds)]

    def on_device(fields, land_sea, topography, land_embed, topography_embed, offsets, gains, w_qkv, w_out, w_up, w_down, bias):
        sec, lon = lax.axis_index("section"), lax.axis_index("lon")
        kind, core = lon // ring, lon % 2
        classes = land_embed.shape[0] + topography_embed.shape[0]
        spare = PAD - C

        ints = jnp.stack([kind, core]).astype(jnp.int32)
        half = jax.ShapeDtypeStruct((C, 4 * C), BF)
        full = jax.ShapeDtypeStruct((2, C, 4 * C), BF)
        own_a, own_b, send_a, send_b = call(pack_kernel, "pack", [SM] + [VM] * 6, [full, full, half, half])(
            ints, w_qkv[0], w_out[0], w_up[0], w_down[0], gains[0], bias[0]
        )
        partner = [(i, i ^ 1) for i in range(strips)]
        cands = []
        for k in range(1, sections):
            perm = [(i, i ^ k) for i in range(sections)]
            mine_a = lax.ppermute(send_a, "section", perm)
            mine_b = lax.ppermute(send_b, "section", perm)
            other_a = lax.ppermute(mine_a, "lon", partner)
            other_b = lax.ppermute(mine_b, "lon", partner)
            cands += [mine_a, mine_b, other_a, other_b]

        def weights_of(b):
            pick = jnp.stack([sec ^ b, core]).astype(jnp.int32)
            return call(
                functools.partial(collect_kernel, sections),
                "collect",
                [SM] + [ANY] * (2 + len(cands)),
                [
                    jax.ShapeDtypeStruct((C, 4 * PAD), BF),
                    jax.ShapeDtypeStruct((C, 4 * C), BF),
                    jax.ShapeDtypeStruct((4 * C, C), BF),
                    jax.ShapeDtypeStruct((WTOK, LANE * (HEADS + 1)), BF),
                    jax.ShapeDtypeStruct((2, C), BF),
                ],
                [pltpu.VMEM((4, C, 4 * C), BF), pltpu.SemaphoreType.DMA],
            )(pick, own_a, own_b, *cands)

        table = jnp.concatenate([land_embed, topography_embed], axis=0)
        table = jnp.pad(table, ((LANE - spare, spare - classes), (0, 0)))

        cls = jnp.arange(spare, dtype=jnp.int32)
        hot = (land_sea[..., None] == cls) | (topography[..., None] + land_embed.shape[0] == cls)
        hot = jnp.broadcast_to(hot.astype(BF)[None], (WL, WT, WN, spare)).reshape(WTOK, spare)
        levels = fields.reshape(kinds, WTOK, C)
        got = []
        for turn in range(2):
            piece = lax.dynamic_index_in_dim(levels, (core + turn) % 2, 0, keepdims=False)
            piece = jnp.concatenate([piece, hot], axis=1)
            perm = [(j, place[(j + turn) % 2][j // 2]) for j in range(strips)]
            got.append(lax.ppermute(piece, "lon", perm))
        w0 = jnp.where(kind == 0, got[0], got[1])
        w1 = jnp.where(kind == 0, got[1], got[0])

        west = [(place[kd][(r + 1) % ring], place[kd][r]) for kd in range(kinds) for r in range(ring)]
        ready = [[*weights_of(b), table] for b in range(sections)]
        frame = jnp.int32(0)
        for t in range(STEPS * sections):
            b = t % sections
            delta = (offsets[b] - frame) % WN
            frame = frame + delta
            d = delta.reshape(1)
            edge = lax.ppermute(w0, "lon", west)
            n0 = block(b == 0, d, w0, w1, ready[b])
            n1 = block(b == 0, d, w1, edge, ready[b])
            w0, w1 = n0, n1

        def send_home(turn):
            def go(w0, w1):
                out = []
                for slot, w in enumerate((w0, w1)):
                    for role in range(2):
                        perm = []
                        for kd in range(kinds):
                            for r in range(ring):
                                home = 2 * r + slot + turn + (kd ^ role)
                                perm.append((place[kd][r], home % strips))
                        out.append(lax.ppermute(w, "lon", perm))
                return tuple(out)

            return go

        turn = (frame // WN) % strips
        homes = lax.switch(turn, [send_home(q) for q in range(strips)], w0, w1)
        parity = (lon - turn) % 2
        ints = jnp.stack([WN - frame % WN, parity]).astype(jnp.int32)
        out = call(merge_kernel, "merge", [SM] + [VM] * 4, jax.ShapeDtypeStruct((kinds, WTOK, C), BF))(ints, *homes)
        return out.reshape(fields.shape)

    return jax.shard_map(
        on_device,
        mesh=mesh,
        in_specs=(
            P("section", None, None, "lon", None),
            P(None, "lon"),
            P(None, "lon"),
            P(),
            P(),
            P(),
            P("section", None, None),
            P("section", None, None),
            P("section", None, None),
            P("section", None, None),
            P("section", None, None),
            P("section", None, None, None, None),
        ),
        out_specs=P("section", None, None, "lon", None),
        check_vma=False,
    )
```

time: 422 us -> 122 us (0.29)
  waiting for transfers between devices: 215 us -> 21.1 us
  matrix products: 101 us -> 0 us
  Pallas kernels: 0 us -> 41.2 us
  loops' own time: 25 us -> 0.08 us
  starting transfers between devices: 7.11 us -> 31.7 us
  other arithmetic: 13 us -> 0.51 us
  blocking collectives: 11.9 us -> 0 us
  local copies, waits for them, and re-layouts: 30.8 us -> 19.7 us
  between operations: 17 us -> 6.01 us
    ppermute x33 -> x26, waiting for transfers between devices: 171 us -> 21.1 us  [the longest x3 11.2 us: on_device(): mine_a = lax.ppermute(send_a, 'section', perm)]
    dot_general x57 -> x0, matrix products: 65.9 us -> none  [the longest x11 32.3 us: run_block(): jnp.einsum('ltnf,fc->ltnc', activated, w_down, preferred_element_type=jnp...]
    psum x1 -> x0, waiting for transfers between devices: 43.5 us -> none  [spread(): return lax.psum(kept, axis)]
    pallas_call x0 -> x22, Pallas kernels: none -> 41.2 us  [the longest x16 33.4 us: block(): call(functools.partial(block_kernel, first), 'block_first' if first else...]
    sub x11 -> x0, matrix products: 35.1 us -> none  [window_attention(): attn_probs = jax.nn.softmax(scores, axis=-1).astype(jnp.bfloat16)]
    another operation x1, loops' own time: 25 us -> 0.08 us  [on_device(): homes = lax.switch(turn, [send_home(q) for q in range(strips)], w0, w1)]
    ppermute x33 -> x26, starting transfers between devices: 7.11 us -> 31.7 us  [the longest x4 11.9 us: go(): out.append(lax.ppermute(w, 'lon', perm))]
    unnamed x18 -> x130, local copies, waits for them, and re-layouts: 0.05 us -> 18.1 us
  transfers between devices with their start and end apart: 34 -> 26, of which waited for: 34 -> 6; matrix products, arithmetic and copies ran while one was open for 1% -> 1% of each run, Pallas kernels for 0% -> 31%
where the time goes in v1:
time: 122 us; the launch traced here: 120 us
  Pallas kernels  41.2 us (34%)
  starting transfers between devices  31.7 us (26%)
  waiting for transfers between devices  21.1 us (17%)
  local copies, waits for them, and re-layouts  19.7 us (16%)
  between operations  6.01 us (5%)
    pallas_call x16, Pallas kernels, block(): call(functools.partial(block_kernel, first), 'block_first' if first else...  33.4 us
    unnamed x130, local copies, waits for them, and re-layouts  18.1 us
    ppermute x4, starting transfers between devices, go(): out.append(lax.ppermute(w, 'lon', perm))  11.9 us
    ppermute x3, waiting for transfers between devices, on_device(): mine_a = lax.ppermute(send_a, 'section', perm)  11.2 us
    ppermute x3, waiting for transfers between devices, on_device(): mine_b = lax.ppermute(send_b, 'section', perm)  7.31 us
    ppermute x3, starting transfers between devices, on_device(): mine_a = lax.ppermute(send_a, 'section', perm)  6.94 us
    ppermute x2, starting transfers between devices, on_device(): got.append(lax.ppermute(piece, 'lon', perm))  5.08 us
    pallas_call x4, Pallas kernels, weights_of(): call(functools.partial(collect_kernel, sections), 'collect', [SM] + [ANY]...  5.04 us
  transfers between devices with their start and end apart: 26, of which 6 were waited for; matrix products, arithmetic and copies ran while one was open for 1% of the time, Pallas kernels for 31%

profile of v1, /device:TPU:0, one launch (start us, length us, event | category | flops | bytes accessed | tf_op | source)
XLA Modules:
  0.0 120.2 jit_solution(3429075478855623546)
XLA Ops:
  3.2 1.5 %pack.1 = (bf16[2,192,768]{2,1,0:T(8,128)(2,1)S(1)}, bf16[2,192,768]{2,1,0:T(8,128)(2,1)S(1)}, bf16[192,768]{1,0:T(8,128)(2,1)}, bf16[192,768]{1,0:T(8,128)(2,1)}) custom-call(s32[2]{0:T(128)S(1)} %pad_add_fusion.2.i_ref, bf16[192,576]{1,0:T(8,128)(2,1)S(1)} %bitcast.33, bf16[192,192]{1,0:T(8,128)(2,1)S(1)} %bitcast.34, bf16[192,768]{1,0:T(8,128)(2,1)S(1)} %bitcast.32, ...), custom_call_target="tpu_custom_call" | custom-call | tf_op jit(solution)/shard_map/pack/pallas_call | solution.py:215
  4.7 3.0 %collective-permute-start.34 = (bf16[192,768]{1,0:T(8,128)(2,1)}, bf16[192,768]{1,0:T(8,128)(2,1)S(1)}, u32[]{:S(2)}, u32[]{:S(2)}) collective-permute-start(bf16[192,768]{1,0:T(8,128)(2,1)} %get-tuple-element.83), channel_id=1, source_target_pairs={{0,8},{8,0},{16,24},{24,16},{1,9},{9,1},{17,25},{25,17},{2,10},{10... | collective-permute-start | bytes 884744 | tf_op jit(solution)/shard_map/ppermute | solution.py:222
  10.0 4.4 %collective-permute-start.33 = (bf16[144,256]{1,0:T(8,128)(2,1)S(1)}, bf16[144,256]{1,0:T(8,128)(2,1)S(1)}, u32[]{:S(2)}, u32[]{:S(2)}) collective-permute-start(bf16[144,256]{1,0:T(8,128)(2,1)S(1)} %get-tuple-element.113), channel_id=1, source_target_pairs={{0,4},{1,0},{2,6},{3,2},{4,7},{5,3},{6,5},{7,1},{8,12},{9,8},{10,1... | collective-permute-start | bytes 221192 | tf_op jit(solution)/shard_map/ppermute | solution.py:256
  14.5 1.5 %collective-permute-start.38 = (bf16[192,768]{1,0:T(8,128)(2,1)}, bf16[192,768]{1,0:T(8,128)(2,1)S(1)}, u32[]{:S(2)}, u32[]{:S(2)}) collective-permute-start(bf16[192,768]{1,0:T(8,128)(2,1)} %get-tuple-element.83), channel_id=1, source_target_pairs={{0,16},{8,24},{16,0},{24,8},{1,17},{9,25},{17,1},{25,9},{2,18},{10... | collective-permute-start | bytes 884744 | tf_op jit(solution)/shard_map/ppermute | solution.py:222
  16.5 2.4 %collective-permute-start.42 = (bf16[192,768]{1,0:T(8,128)(2,1)}, bf16[192,768]{1,0:T(8,128)(2,1)S(1)}, u32[]{:S(2)}, u32[]{:S(2)}) collective-permute-start(bf16[192,768]{1,0:T(8,128)(2,1)} %get-tuple-element.83), channel_id=1, source_target_pairs={{0,24},{8,16},{16,8},{24,0},{1,25},{9,17},{17,9},{25,1},{2,26},{10... | collective-permute-start | bytes 884744 | tf_op jit(solution)/shard_map/ppermute | solution.py:222
  19.4 1.8 %collective-permute-done.35.refs_1_ = bf16[192,768]{1,0:T(8,128)(2,1)S(1)} collective-permute-done((bf16[192,768]{1,0:T(8,128)(2,1)}, bf16[192,768]{1,0:T(8,128)(2,1)S(1)}, u32[]{:S(2)}, u32[]{:S(2)}) %collective-permute-start.35) | collective-permute-done | bytes 294944 | tf_op jit(solution)/shard_map/ppermute | solution.py:223
  26.0 11.2 %collective-permute-done.38.refs_4_ = bf16[192,768]{1,0:T(8,128)(2,1)S(1)} collective-permute-done((bf16[192,768]{1,0:T(8,128)(2,1)}, bf16[192,768]{1,0:T(8,128)(2,1)S(1)}, u32[]{:S(2)}, u32[]{:S(2)}) %collective-permute-start.38) | collective-permute-done | bytes 294944 | tf_op jit(solution)/shard_map/ppermute | solution.py:222
  37.2 5.5 %collective-permute-done.39.refs_5_ = bf16[192,768]{1,0:T(8,128)(2,1)S(1)} collective-permute-done((bf16[192,768]{1,0:T(8,128)(2,1)}, bf16[192,768]{1,0:T(8,128)(2,1)S(1)}, u32[]{:S(2)}, u32[]{:S(2)}) %collective-permute-start.39) | collective-permute-done | bytes 294944 | tf_op jit(solution)/shard_map/ppermute | solution.py:223
  48.0 1.9 %block_first.4.a_ref = bf16[144,256]{1,0:T(8,128)(2,1)S(1)} custom-call(s32[1]{0:T(128)} %bitcast.13.d_ref, bf16[144,256]{1,0:T(8,128)(2,1)S(1)} %get-tuple-element.110.a_ref, bf16[144,256]{1,0:T(8,128)(2,1)S(1)} %get-tuple-element.109.b_ref.a_ref, bf16[192,1024]{1,0:T(8,128)(2,1)S(1)} %get-tuple-element.85.wp_ref, ...), custom_call_target="tpu_custom_call" | custom-call | tf_op jit(solution)/shard_map/block_first/pallas_call | solution.py:120
  49.9 1.2 %collective-permute-start.47 = (bf16[144,256]{1,0:T(8,128)(2,1)S(1)}, bf16[144,256]{1,0:T(8,128)(2,1)S(1)}, u32[]{:S(2)}, u32[]{:S(2)}) collective-permute-start(bf16[144,256]{1,0:T(8,128)(2,1)S(1)} %block_first.4.a_ref), channel_id=1, source_target_pairs={{2,0},{3,2},{1,3},{0,1},{6,4},{7,6},{5,7},{4,5},{10,8},{11,10},{9,... | collective-permute-start | bytes 221192 | tf_op jit(solution)/shard_map/ppermute | solution.py:268
  51.2 1.8 %collect.5 = (bf16[192,1024]{1,0:T(8,128)(2,1)S(1)}, bf16[192,768]{1,0:T(8,128)(2,1)S(1)}, bf16[768,192]{1,0:T(8,128)(2,1)S(1)}, bf16[144,896]{1,0:T(8,128)(2,1)S(1)}, bf16[2,192]{1,0:T(2,128)(2,1)S(1)}) custom-call(s32[2]{0:T(128)S(1)} %get-tuple-element.120.i_ref, bf16[2,192,768]{2,1,0:T(8,128)(2,1)S(1)} %get-tuple-element.81.own_a, ...), custom_call_target="tpu_custom_call" | custom-call | tf_op jit(solution)/shard_map/collect/pallas_call | solution.py:230
  53.0 1.9 %block_first.5.b_ref.a_ref = bf16[144,256]{1,0:T(8,128)(2,1)S(1)} custom-call(s32[1]{0:T(128)} %bitcast.13.d_ref, bf16[144,256]{1,0:T(8,128)(2,1)S(1)} %get-tuple-element.109.b_ref.a_ref, bf16[144,256]{1,0:T(8,128)(2,1)S(1)} %collective-permute-done.46.b_ref, bf16[192,1024]{1,0:T(8,128)(2,1)S(1)} %get-tuple-element.85.wp_ref, ...), custom_call_target="tpu_custom_call" | custom-call | tf_op jit(solution)/shard_map/block_first/pallas_call | solution.py:120
  54.9 2.4 %block.12.a_ref = bf16[144,256]{1,0:T(8,128)(2,1)} custom-call(s32[1]{0:T(128)} %bitcast.12.d_ref, bf16[144,256]{1,0:T(8,128)(2,1)S(1)} %block_first.4.a_ref, bf16[144,256]{1,0:T(8,128)(2,1)S(1)} %block_first.5.b_ref.a_ref, bf16[192,1024]{1,0:T(8,128)(2,1)S(1)} %get-tuple-element.90.wp_ref, bf16[192,768]{1,0:T(8,128)(2,1)S(1)} %get-tuple-element.91.up_ref, ...), custom_call_target="tpu_custom_call" | custom-call | tf_op jit(solution)/shard_map/block/pallas_call | solution.py:120
  59.0 1.8 %block.13.b_ref.a_ref = bf16[144,256]{1,0:T(8,128)(2,1)S(1)} custom-call(s32[1]{0:T(128)} %bitcast.12.d_ref, bf16[144,256]{1,0:T(8,128)(2,1)S(1)} %block_first.5.b_ref.a_ref, bf16[144,256]{1,0:T(8,128)(2,1)S(1)} %collective-permute-done.47.b_ref, bf16[192,1024]{1,0:T(8,128)(2,1)S(1)} %get-tuple-element.90.wp_ref, ...), custom_call_target="tpu_custom_call" | custom-call | tf_op jit(solution)/shard_map/block/pallas_call | solution.py:120
  60.8 3.3 %block.14.a_ref = bf16[144,256]{1,0:T(8,128)(2,1)} custom-call(s32[1]{0:T(128)} %bitcast.11.d_ref, bf16[144,256]{1,0:T(8,128)(2,1)} %block.12.a_ref, bf16[144,256]{1,0:T(8,128)(2,1)S(1)} %block.13.b_ref.a_ref, bf16[192,1024]{1,0:T(8,128)(2,1)S(1)} %get-tuple-element.95.wp_ref, bf16[192,768]{1,0:T(8,128)(2,1)S(1)} %get-tuple-element.96.up_ref, ...), custom_call_target="tpu_custom_call" | custom-call | tf_op jit(solution)/shard_map/block/pallas_call | solution.py:120
  76.6 2.7 %block.15.b_ref.a_ref = bf16[144,256]{1,0:T(8,128)(2,1)S(1)} custom-call(s32[1]{0:T(128)} %bitcast.11.d_ref, bf16[144,256]{1,0:T(8,128)(2,1)S(1)} %copy-done.53, bf16[144,256]{1,0:T(8,128)(2,1)} %collective-permute-done.48.b_ref, bf16[192,1024]{1,0:T(8,128)(2,1)S(1)} %get-tuple-element.95.wp_ref, bf16[192,768]{1,0:T(8,128)(2,1)S(1)} %copy-done.38, ...), custom_call_target="tpu_custom_call" | custom-call | tf_op jit(solution)/shard_map/block/pallas_call | solution.py:120
  79.3 2.6 %block.16.a_ref = bf16[144,256]{1,0:T(8,128)(2,1)S(1)} custom-call(s32[1]{0:T(128)} %bitcast.10.d_ref, bf16[144,256]{1,0:T(8,128)(2,1)} %block.14.a_ref, bf16[144,256]{1,0:T(8,128)(2,1)S(1)} %block.15.b_ref.a_ref, bf16[192,1024]{1,0:T(8,128)(2,1)S(1)} %get-tuple-element.100.wp_ref, bf16[192,768]{1,0:T(8,128)(2,1)S(1)} %get-tuple-element.101.up_ref, ...), custom_call_target="tpu_custom_call" | custom-call | tf_op jit(solution)/shard_map/block/pallas_call | solution.py:120
  82.3 2.6 %block.17.b_ref.a_ref = bf16[144,256]{1,0:T(8,128)(2,1)S(1)} custom-call(s32[1]{0:T(128)} %bitcast.10.d_ref, bf16[144,256]{1,0:T(8,128)(2,1)S(1)} %block.15.b_ref.a_ref, bf16[144,256]{1,0:T(8,128)(2,1)} %collective-permute-done.49.b_ref, bf16[192,1024]{1,0:T(8,128)(2,1)S(1)} %get-tuple-element.100.wp_ref, bf16[192,768]{1,0:T(8,128)(2,1)S(1)} %get-tuple-element.101.up_ref, ...), custom_call_target="tpu_custom_call" | custom-call | tf_op jit(solution)/shard_map/block/pallas_call | solution.py:120
  84.9 1.9 %block_first.6.a_ref = bf16[144,256]{1,0:T(8,128)(2,1)S(1)} custom-call(s32[1]{0:T(128)} %bitcast.9.d_ref, bf16[144,256]{1,0:T(8,128)(2,1)S(1)} %block.16.a_ref, bf16[144,256]{1,0:T(8,128)(2,1)S(1)} %block.17.b_ref.a_ref, bf16[192,1024]{1,0:T(8,128)(2,1)S(1)} %get-tuple-element.85.wp_ref, bf16[192,768]{1,0:T(8,128)(2,1)S(1)} %copy-done.34, ...), custom_call_target="tpu_custom_call" | custom-call | tf_op jit(solution)/shard_map/block_first/pallas_call | solution.py:120
  90.0 1.9 %block_first.7.b_ref.a_ref = bf16[144,256]{1,0:T(8,128)(2,1)S(1)} custom-call(s32[1]{0:T(128)} %bitcast.9.d_ref, bf16[144,256]{1,0:T(8,128)(2,1)S(1)} %block.17.b_ref.a_ref, bf16[144,256]{1,0:T(8,128)(2,1)S(1)} %collective-permute-done.50.b_ref, bf16[192,1024]{1,0:T(8,128)(2,1)S(1)} %get-tuple-element.85.wp_ref, bf16[192,768]{1,0:T(8,128)(2,1)S(1)} %copy-done.34, ...), custom_call_target="tpu_custom_call" | custom-call | tf_op jit(solution)/shard_map/block_first/pallas_call | solution.py:120
  91.9 1.7 %block.18.a_ref = bf16[144,256]{1,0:T(8,128)(2,1)S(1)} custom-call(s32[1]{0:T(128)} %bitcast.8.d_ref, bf16[144,256]{1,0:T(8,128)(2,1)S(1)} %block_first.6.a_ref, bf16[144,256]{1,0:T(8,128)(2,1)S(1)} %block_first.7.b_ref.a_ref, bf16[192,1024]{1,0:T(8,128)(2,1)S(1)} %get-tuple-element.90.wp_ref, bf16[192,768]{1,0:T(8,128)(2,1)S(1)} %copy-done.36, ...), custom_call_target="tpu_custom_call" | custom-call | tf_op jit(solution)/shard_map/block/pallas_call | solution.py:120
  94.3 1.7 %block.19.b_ref.a_ref = bf16[144,256]{1,0:T(8,128)(2,1)S(1)} custom-call(s32[1]{0:T(128)} %bitcast.8.d_ref, bf16[144,256]{1,0:T(8,128)(2,1)S(1)} %block_first.7.b_ref.a_ref, bf16[144,256]{1,0:T(8,128)(2,1)S(1)} %collective-permute-done.51.b_ref, bf16[192,1024]{1,0:T(8,128)(2,1)S(1)} %get-tuple-element.90.wp_ref, bf16[192,768]{1,0:T(8,128)(2,1)S(1)} %copy-done.36, ...), custom_call_target="tpu_custom_call" | custom-call | tf_op jit(solution)/shard_map/block/pallas_call | solution.py:120
  96.1 1.7 %block.20.a_ref = bf16[144,256]{1,0:T(8,128)(2,1)S(1)} custom-call(s32[1]{0:T(128)} %bitcast.7.d_ref, bf16[144,256]{1,0:T(8,128)(2,1)S(1)} %block.18.a_ref, bf16[144,256]{1,0:T(8,128)(2,1)S(1)} %block.19.b_ref.a_ref, bf16[192,1024]{1,0:T(8,128)(2,1)S(1)} %get-tuple-element.95.wp_ref, bf16[192,768]{1,0:T(8,128)(2,1)S(1)} %copy-done.39, ...), custom_call_target="tpu_custom_call" | custom-call | tf_op jit(solution)/shard_map/block/pallas_call | solution.py:120
  98.6 1.7 %block.21.b_ref.a_ref = bf16[144,256]{1,0:T(8,128)(2,1)S(1)} custom-call(s32[1]{0:T(128)} %bitcast.7.d_ref, bf16[144,256]{1,0:T(8,128)(2,1)S(1)} %block.19.b_ref.a_ref, bf16[144,256]{1,0:T(8,128)(2,1)S(1)} %collective-permute-done.52.b_ref, bf16[192,1024]{1,0:T(8,128)(2,1)S(1)} %get-tuple-element.95.wp_ref, bf16[192,768]{1,0:T(8,128)(2,1)S(1)} %copy-done.39, ...), custom_call_target="tpu_custom_call" | custom-call | tf_op jit(solution)/shard_map/block/pallas_call | solution.py:120
  100.4 1.7 %block.22 = bf16[144,256]{1,0:T(8,128)(2,1)S(1)} custom-call(s32[1]{0:T(128)} %bitcast.6.d_ref, bf16[144,256]{1,0:T(8,128)(2,1)S(1)} %block.20.a_ref, bf16[144,256]{1,0:T(8,128)(2,1)S(1)} %block.21.b_ref.a_ref, bf16[192,1024]{1,0:T(8,128)(2,1)S(1)} %copy-done.4, bf16[192,768]{1,0:T(8,128)(2,1)S(1)} %copy-done.41, bf16[768,192]{1,0:T(8,128)(2,1)S(1)} %copy-done.6, ...), custom_call_target="tpu_custom_call" | custom-call | tf_op jit(solution)/shard_map/block/pallas_call | solution.py:120
  102.5 1.7 %block.23 = bf16[144,256]{1,0:T(8,128)(2,1)S(1)} custom-call(s32[1]{0:T(128)} %bitcast.6.d_ref, bf16[144,256]{1,0:T(8,128)(2,1)S(1)} %block.21.b_ref.a_ref, bf16[144,256]{1,0:T(8,128)(2,1)S(1)} %collective-permute-done.53.b_ref, bf16[192,1024]{1,0:T(8,128)(2,1)S(1)} %copy-done.4, bf16[192,768]{1,0:T(8,128)(2,1)S(1)} %copy-done.41, ...), custom_call_target="tpu_custom_call" | custom-call | tf_op jit(solution)/shard_map/block/pallas_call | solution.py:120
  104.2 14.0 %conditional.1 = (bf16[144,256]{1,0:T(8,128)(2,1)}, bf16[144,256]{1,0:T(8,128)(2,1)}, bf16[144,256]{1,0:T(8,128)(2,1)}, bf16[144,256]{1,0:T(8,128)(2,1)}) conditional(s32[]{:T(128)} %clamp.3, (bf16[144,256]{1,0:T(8,128)(2,1)S(1)}, bf16[144,256]{1,0:T(8,128)(2,1)S(1)}) %tuple.37, (bf16[144,256]{1,0:T(8,128)(2,1)S(1)}, ...), branch_computations={%region_0.1_spmd, %region_1.2_spmd, %region_2.3_spmd, %region_3.4_... | conditional | bytes 1179840 | solution.py:289
  104.2 2.8 %collective-permute-start.10 = (bf16[144,256]{1,0:T(8,128)(2,1)S(1)}, bf16[144,256]{1,0:T(8,128)(2,1)}, u32[]{:S(2)}, u32[]{:S(2)}) collective-permute-start(bf16[144,256]{1,0:T(8,128)(2,1)S(1)} %get-tuple-element.42), channel_id=1, source_target_pairs={{0,3},{2,5},{3,7},{1,1},{4,4},{6,6},{7,0},{5,2},{8,11},{10,13},{11... | collective-permute-start | bytes 221192 | tf_op jit(solution)/shard_map/cond/branch_2_fun/ppermute | solution.py:283
  107.1 1.9 %collective-permute-start.11 = (bf16[144,256]{1,0:T(8,128)(2,1)S(1)}, bf16[144,256]{1,0:T(8,128)(2,1)}, u32[]{:S(2)}, u32[]{:S(2)}) collective-permute-start(bf16[144,256]{1,0:T(8,128)(2,1)S(1)} %get-tuple-element.42), channel_id=1, source_target_pairs={{0,4},{2,6},{3,0},{1,2},{4,3},{6,5},{7,7},{5,1},{8,12},{10,14},{11... | collective-permute-start | bytes 221192 | tf_op jit(solution)/shard_map/cond/branch_2_fun/ppermute | solution.py:283
  109.0 2.5 %collective-permute-start.8 = (bf16[144,256]{1,0:T(8,128)(2,1)S(1)}, bf16[144,256]{1,0:T(8,128)(2,1)}, u32[]{:S(2)}, u32[]{:S(2)}) collective-permute-start(bf16[144,256]{1,0:T(8,128)(2,1)S(1)} %get-tuple-element.41), channel_id=1, source_target_pairs={{0,2},{2,4},{3,6},{1,0},{4,3},{6,5},{7,7},{5,1},{8,10},{10,12},{11... | collective-permute-start | bytes 221192 | tf_op jit(solution)/shard_map/cond/branch_2_fun/ppermute | solution.py:283
  111.5 4.7 %collective-permute-start.9 = (bf16[144,256]{1,0:T(8,128)(2,1)S(1)}, bf16[144,256]{1,0:T(8,128)(2,1)}, u32[]{:S(2)}, u32[]{:S(2)}) collective-permute-start(bf16[144,256]{1,0:T(8,128)(2,1)S(1)} %get-tuple-element.41), channel_id=1, source_target_pairs={{0,3},{2,5},{3,7},{1,1},{4,2},{6,4},{7,6},{5,0},{8,11},{10,13},{11... | collective-permute-start | bytes 221192 | tf_op jit(solution)/shard_map/cond/branch_2_fun/ppermute | solution.py:283
  116.2 2.0 %collective-permute-done.9 = bf16[144,256]{1,0:T(8,128)(2,1)} collective-permute-done((bf16[144,256]{1,0:T(8,128)(2,1)S(1)}, bf16[144,256]{1,0:T(8,128)(2,1)}, u32[]{:S(2)}, u32[]{:S(2)}) %collective-permute-start.9) | collective-permute-done | bytes 73760 | tf_op jit(solution)/shard_map/cond/branch_2_fun/ppermute | solution.py:283
  (189 shorter events, 32.4 us)
Async XLA Ops:
  4.7 14.2 %collective-permute-start.34 = (bf16[192,768]{1,0:T(8,128)(2,1)}, bf16[192,768]{1,0:T(8,128)(2,1)S(1)}, u32[]{:S(2)}, u32[]{:S(2)}) collective-permute-start(bf16[192,768]{1,0:T(8,128)(2,1)} %get-tuple-element.83), channel_id=1, source_target_pairs={{0,8},{8,0},{16,24},{24,16},{1,9},{9,1},{17,25},{25,17},{2,10},{10... | collective-permute-start | bytes 884744 | tf_op jit(solution)/shard_map/ppermute | solution.py:222
  7.7 13.5 %collective-permute-start.35 = (bf16[192,768]{1,0:T(8,128)(2,1)}, bf16[192,768]{1,0:T(8,128)(2,1)S(1)}, u32[]{:S(2)}, u32[]{:S(2)}) collective-permute-start(bf16[192,768]{1,0:T(8,128)(2,1)} %get-tuple-element.84), channel_id=1, source_target_pairs={{0,8},{8,0},{16,24},{24,16},{1,9},{9,1},{17,25},{25,17},{2,10},{10... | collective-permute-start | bytes 884744 | tf_op jit(solution)/shard_map/ppermute | solution.py:223
  9.4 6.6 %collective-permute-start.32 = (bf16[144,256]{1,0:T(8,128)(2,1)S(1)}, bf16[144,256]{1,0:T(8,128)(2,1)S(1)}, u32[]{:S(2)}, u32[]{:S(2)}) collective-permute-start(bf16[144,256]{1,0:T(8,128)(2,1)S(1)} %get-tuple-element.114), channel_id=1, source_target_pairs={{0,0},{1,4},{2,2},{3,6},{4,3},{5,7},{6,1},{7,5},{8,8},{9,12},{10,1... | collective-permute-start | bytes 221192 | tf_op jit(solution)/shard_map/ppermute | solution.py:256
  10.0 6.5 %collective-permute-start.33 = (bf16[144,256]{1,0:T(8,128)(2,1)S(1)}, bf16[144,256]{1,0:T(8,128)(2,1)S(1)}, u32[]{:S(2)}, u32[]{:S(2)}) collective-permute-start(bf16[144,256]{1,0:T(8,128)(2,1)S(1)} %get-tuple-element.113), channel_id=1, source_target_pairs={{0,4},{1,0},{2,6},{3,2},{4,7},{5,3},{6,5},{7,1},{8,12},{9,8},{10,1... | collective-permute-start | bytes 221192 | tf_op jit(solution)/shard_map/ppermute | solution.py:256
  14.5 22.7 %collective-permute-start.38 = (bf16[192,768]{1,0:T(8,128)(2,1)}, bf16[192,768]{1,0:T(8,128)(2,1)S(1)}, u32[]{:S(2)}, u32[]{:S(2)}) collective-permute-start(bf16[192,768]{1,0:T(8,128)(2,1)} %get-tuple-element.83), channel_id=1, source_target_pairs={{0,16},{8,24},{16,0},{24,8},{1,17},{9,25},{17,1},{25,9},{2,18},{10... | collective-permute-start | bytes 884744 | tf_op jit(solution)/shard_map/ppermute | solution.py:222
  16.0 26.7 %collective-permute-start.39 = (bf16[192,768]{1,0:T(8,128)(2,1)}, bf16[192,768]{1,0:T(8,128)(2,1)S(1)}, u32[]{:S(2)}, u32[]{:S(2)}) collective-permute-start(bf16[192,768]{1,0:T(8,128)(2,1)} %get-tuple-element.84), channel_id=1, source_target_pairs={{0,16},{8,24},{16,0},{24,8},{1,17},{9,25},{17,1},{25,9},{2,18},{10... | collective-permute-start | bytes 884744 | tf_op jit(solution)/shard_map/ppermute | solution.py:223
  16.5 26.2 %collective-permute-start.42 = (bf16[192,768]{1,0:T(8,128)(2,1)}, bf16[192,768]{1,0:T(8,128)(2,1)S(1)}, u32[]{:S(2)}, u32[]{:S(2)}) collective-permute-start(bf16[192,768]{1,0:T(8,128)(2,1)} %get-tuple-element.83), channel_id=1, source_target_pairs={{0,24},{8,16},{16,8},{24,0},{1,25},{9,17},{17,9},{25,1},{2,26},{10... | collective-permute-start | bytes 884744 | tf_op jit(solution)/shard_map/ppermute | solution.py:222
  19.0 24.3 %collective-permute-start.43 = (bf16[192,768]{1,0:T(8,128)(2,1)}, bf16[192,768]{1,0:T(8,128)(2,1)S(1)}, u32[]{:S(2)}, u32[]{:S(2)}) collective-permute-start(bf16[192,768]{1,0:T(8,128)(2,1)} %get-tuple-element.84), channel_id=1, source_target_pairs={{0,24},{8,16},{16,8},{24,0},{1,25},{9,17},{17,9},{25,1},{2,26},{10... | collective-permute-start | bytes 884744 | tf_op jit(solution)/shard_map/ppermute | solution.py:223
  21.2 30.0 %copy-start.7 = (bf16[192,768]{1,0:T(8,128)(2,1)}, bf16[192,768]{1,0:T(8,128)(2,1)S(1)}, u32[]{:S(2)}) copy-start(bf16[192,768]{1,0:T(8,128)(2,1)S(1)} %collective-permute-done.35.refs_1_) | copy-start | bytes 884740
  21.2 22.8 %collective-permute-start.36 = (bf16[192,768]{1,0:T(8,128)(2,1)S(1)}, bf16[192,768]{1,0:T(8,128)(2,1)}, u32[]{:S(2)}, u32[]{:S(2)}) collective-permute-start(bf16[192,768]{1,0:T(8,128)(2,1)S(1)} %collective-permute-done.34.refs_0_), channel_id=1, source_target_pairs={{0,1},{1,0},{2,3},{3,2},{4,5},{5,4},{6,7},{7,6},{8,9},{9,8},{10,11... | collective-permute-start | bytes 884744 | tf_op jit(solution)/shard_map/ppermute | solution.py:224
  37.2 8.1 %collective-permute-start.37 = (bf16[192,768]{1,0:T(8,128)(2,1)S(1)}, bf16[192,768]{1,0:T(8,128)(2,1)S(1)}, u32[]{:S(2)}, u32[]{:S(2)}) collective-permute-start(bf16[192,768]{1,0:T(8,128)(2,1)S(1)} %collective-permute-done.35.refs_1_), channel_id=1, source_target_pairs={{0,1},{1,0},{2,3},{3,2},{4,5},{5,4},{6,7},{7,6},{8,9},{9,8},{10,11... | collective-permute-start | bytes 884744 | tf_op jit(solution)/shard_map/ppermute | solution.py:225
  42.7 2.7 %collective-permute-start.40 = (bf16[192,768]{1,0:T(8,128)(2,1)S(1)}, bf16[192,768]{1,0:T(8,128)(2,1)S(1)}, u32[]{:S(2)}, u32[]{:S(2)}) collective-permute-start(bf16[192,768]{1,0:T(8,128)(2,1)S(1)} %collective-permute-done.38.refs_4_), channel_id=1, source_target_pairs={{0,1},{1,0},{2,3},{3,2},{4,5},{5,4},{6,7},{7,6},{8,9},{9,8},{10,11... | collective-permute-start | bytes 884744 | tf_op jit(solution)/shard_map/ppermute | solution.py:224
  42.7 2.7 %collective-permute-start.41 = (bf16[192,768]{1,0:T(8,128)(2,1)S(1)}, bf16[192,768]{1,0:T(8,128)(2,1)S(1)}, u32[]{:S(2)}, u32[]{:S(2)}) collective-permute-start(bf16[192,768]{1,0:T(8,128)(2,1)S(1)} %collective-permute-done.39.refs_5_), channel_id=1, source_target_pairs={{0,1},{1,0},{2,3},{3,2},{4,5},{5,4},{6,7},{7,6},{8,9},{9,8},{10,11... | collective-permute-start | bytes 884744 | tf_op jit(solution)/shard_map/ppermute | solution.py:225
  43.3 2.2 %collective-permute-start.44 = (bf16[192,768]{1,0:T(8,128)(2,1)S(1)}, bf16[192,768]{1,0:T(8,128)(2,1)S(1)}, u32[]{:S(2)}, u32[]{:S(2)}) collective-permute-start(bf16[192,768]{1,0:T(8,128)(2,1)S(1)} %collective-permute-done.42.refs_8_), channel_id=1, source_target_pairs={{0,1},{1,0},{2,3},{3,2},{4,5},{5,4},{6,7},{7,6},{8,9},{9,8},{10,11... | collective-permute-start | bytes 884744 | tf_op jit(solution)/shard_map/ppermute | solution.py:224
  44.1 1.6 %collective-permute-start.45 = (bf16[192,768]{1,0:T(8,128)(2,1)S(1)}, bf16[192,768]{1,0:T(8,128)(2,1)S(1)}, u32[]{:S(2)}, u32[]{:S(2)}) collective-permute-start(bf16[192,768]{1,0:T(8,128)(2,1)S(1)} %collective-permute-done.43.refs_9_), channel_id=1, source_target_pairs={{0,1},{1,0},{2,3},{3,2},{4,5},{5,4},{6,7},{7,6},{8,9},{9,8},{10,11... | collective-permute-start | bytes 884744 | tf_op jit(solution)/shard_map/ppermute | solution.py:225
  45.3 12.5 %copy-start.23 = (bf16[192,768]{1,0:T(8,128)(2,1)}, bf16[192,768]{1,0:T(8,128)(2,1)S(1)}, u32[]{:S(2)}) copy-start(bf16[192,768]{1,0:T(8,128)(2,1)S(1)} %collective-permute-done.37.refs_3_) | copy-start | bytes 884740
  45.3 7.7 %collective-permute-start.46 = (bf16[144,256]{1,0:T(8,128)(2,1)S(1)}, bf16[144,256]{1,0:T(8,128)(2,1)S(1)}, u32[]{:S(2)}, u32[]{:S(2)}) collective-permute-start(bf16[144,256]{1,0:T(8,128)(2,1)S(1)} %get-tuple-element.110.a_ref), channel_id=1, source_target_pairs={{2,0},{3,2},{1,3},{0,1},{6,4},{7,6},{5,7},{4,5},{10,8},{11,10},{9,... | collective-permute-start | bytes 221192 | tf_op jit(solution)/shard_map/ppermute | solution.py:268
  45.5 12.4 %copy-start.25 = (bf16[192,768]{1,0:T(8,128)(2,1)}, bf16[192,768]{1,0:T(8,128)(2,1)S(1)}, u32[]{:S(2)}) copy-start(bf16[192,768]{1,0:T(8,128)(2,1)S(1)} %collective-permute-done.40.refs_6_) | copy-start | bytes 884740
  45.5 12.4 %copy-start.27 = (bf16[192,768]{1,0:T(8,128)(2,1)}, bf16[192,768]{1,0:T(8,128)(2,1)S(1)}, u32[]{:S(2)}) copy-start(bf16[192,768]{1,0:T(8,128)(2,1)S(1)} %collective-permute-done.41.refs_7_) | copy-start | bytes 884740
  45.5 12.3 %copy-start.29 = (bf16[192,768]{1,0:T(8,128)(2,1)}, bf16[192,768]{1,0:T(8,128)(2,1)S(1)}, u32[]{:S(2)}) copy-start(bf16[192,768]{1,0:T(8,128)(2,1)S(1)} %collective-permute-done.44.refs_10_) | copy-start | bytes 884740
  45.7 12.1 %copy-start.31 = (bf16[192,768]{1,0:T(8,128)(2,1)}, bf16[192,768]{1,0:T(8,128)(2,1)S(1)}, u32[]{:S(2)}) copy-start(bf16[192,768]{1,0:T(8,128)(2,1)S(1)} %collective-permute-done.45.refs_11_) | copy-start | bytes 884740
  49.9 9.1 %collective-permute-start.47 = (bf16[144,256]{1,0:T(8,128)(2,1)S(1)}, bf16[144,256]{1,0:T(8,128)(2,1)S(1)}, u32[]{:S(2)}, u32[]{:S(2)}) collective-permute-start(bf16[144,256]{1,0:T(8,128)(2,1)S(1)} %block_first.4.a_ref), channel_id=1, source_target_pairs={{2,0},{3,2},{1,3},{0,1},{6,4},{7,6},{5,7},{4,5},{10,8},{11,10},{9,... | collective-permute-start | bytes 221192 | tf_op jit(solution)/shard_map/ppermute | solution.py:268
  57.3 19.2 %collective-permute-start.48 = (bf16[144,256]{1,0:T(8,128)(2,1)}, bf16[144,256]{1,0:T(8,128)(2,1)}, u32[]{:S(2)}, u32[]{:S(2)}) collective-permute-start(bf16[144,256]{1,0:T(8,128)(2,1)} %block.12.a_ref), channel_id=1, source_target_pairs={{2,0},{3,2},{1,3},{0,1},{6,4},{7,6},{5,7},{4,5},{10,8},{11,10},{9,... | collective-permute-start | bytes 221192 | tf_op jit(solution)/shard_map/ppermute | solution.py:268
  64.0 18.2 %collective-permute-start.49 = (bf16[144,256]{1,0:T(8,128)(2,1)}, bf16[144,256]{1,0:T(8,128)(2,1)}, u32[]{:S(2)}, u32[]{:S(2)}) collective-permute-start(bf16[144,256]{1,0:T(8,128)(2,1)} %block.14.a_ref), channel_id=1, source_target_pairs={{2,0},{3,2},{1,3},{0,1},{6,4},{7,6},{5,7},{4,5},{10,8},{11,10},{9,... | collective-permute-start | bytes 221192 | tf_op jit(solution)/shard_map/ppermute | solution.py:268
  82.0 8.0 %collective-permute-start.50 = (bf16[144,256]{1,0:T(8,128)(2,1)S(1)}, bf16[144,256]{1,0:T(8,128)(2,1)S(1)}, u32[]{:S(2)}, u32[]{:S(2)}) collective-permute-start(bf16[144,256]{1,0:T(8,128)(2,1)S(1)} %block.16.a_ref), channel_id=1, source_target_pairs={{2,0},{3,2},{1,3},{0,1},{6,4},{7,6},{5,7},{4,5},{10,8},{11,10},{9,... | collective-permute-start | bytes 221192 | tf_op jit(solution)/shard_map/ppermute | solution.py:268
  86.8 7.5 %collective-permute-start.51 = (bf16[144,256]{1,0:T(8,128)(2,1)S(1)}, bf16[144,256]{1,0:T(8,128)(2,1)S(1)}, u32[]{:S(2)}, u32[]{:S(2)}) collective-permute-start(bf16[144,256]{1,0:T(8,128)(2,1)S(1)} %block_first.6.a_ref), channel_id=1, source_target_pairs={{2,0},{3,2},{1,3},{0,1},{6,4},{7,6},{5,7},{4,5},{10,8},{11,10},{9,... | collective-permute-start | bytes 221192 | tf_op jit(solution)/shard_map/ppermute | solution.py:268
  93.7 4.9 %collective-permute-start.52 = (bf16[144,256]{1,0:T(8,128)(2,1)S(1)}, bf16[144,256]{1,0:T(8,128)(2,1)S(1)}, u32[]{:S(2)}, u32[]{:S(2)}) collective-permute-start(bf16[144,256]{1,0:T(8,128)(2,1)S(1)} %block.18.a_ref), channel_id=1, source_target_pairs={{2,0},{3,2},{1,3},{0,1},{6,4},{7,6},{5,7},{4,5},{10,8},{11,10},{9,... | collective-permute-start | bytes 221192 | tf_op jit(solution)/shard_map/ppermute | solution.py:268
  97.8 4.6 %collective-permute-start.53 = (bf16[144,256]{1,0:T(8,128)(2,1)S(1)}, bf16[144,256]{1,0:T(8,128)(2,1)S(1)}, u32[]{:S(2)}, u32[]{:S(2)}) collective-permute-start(bf16[144,256]{1,0:T(8,128)(2,1)S(1)} %block.20.a_ref), channel_id=1, source_target_pairs={{2,0},{3,2},{1,3},{0,1},{6,4},{7,6},{5,7},{4,5},{10,8},{11,10},{9,... | collective-permute-start | bytes 221192 | tf_op jit(solution)/shard_map/ppermute | solution.py:268
  104.2 11.9 %collective-permute-start.10 = (bf16[144,256]{1,0:T(8,128)(2,1)S(1)}, bf16[144,256]{1,0:T(8,128)(2,1)}, u32[]{:S(2)}, u32[]{:S(2)}) collective-permute-start(bf16[144,256]{1,0:T(8,128)(2,1)S(1)} %get-tuple-element.42), channel_id=1, source_target_pairs={{0,3},{2,5},{3,7},{1,1},{4,4},{6,6},{7,0},{5,2},{8,11},{10,13},{11... | collective-permute-start | bytes 221192 | tf_op jit(solution)/shard_map/cond/branch_2_fun/ppermute | solution.py:283
  107.1 9.1 %collective-permute-start.11 = (bf16[144,256]{1,0:T(8,128)(2,1)S(1)}, bf16[144,256]{1,0:T(8,128)(2,1)}, u32[]{:S(2)}, u32[]{:S(2)}) collective-permute-start(bf16[144,256]{1,0:T(8,128)(2,1)S(1)} %get-tuple-element.42), channel_id=1, source_target_pairs={{0,4},{2,6},{3,0},{1,2},{4,3},{6,5},{7,7},{5,1},{8,12},{10,14},{11... | collective-permute-start | bytes 221192 | tf_op jit(solution)/shard_map/cond/branch_2_fun/ppermute | solution.py:283
  109.0 7.2 %collective-permute-start.8 = (bf16[144,256]{1,0:T(8,128)(2,1)S(1)}, bf16[144,256]{1,0:T(8,128)(2,1)}, u32[]{:S(2)}, u32[]{:S(2)}) collective-permute-start(bf16[144,256]{1,0:T(8,128)(2,1)S(1)} %get-tuple-element.41), channel_id=1, source_target_pairs={{0,2},{2,4},{3,6},{1,0},{4,3},{6,5},{7,7},{5,1},{8,10},{10,12},{11... | collective-permute-start | bytes 221192 | tf_op jit(solution)/shard_map/cond/branch_2_fun/ppermute | solution.py:283
  111.5 6.7 %collective-permute-start.9 = (bf16[144,256]{1,0:T(8,128)(2,1)S(1)}, bf16[144,256]{1,0:T(8,128)(2,1)}, u32[]{:S(2)}, u32[]{:S(2)}) collective-permute-start(bf16[144,256]{1,0:T(8,128)(2,1)S(1)} %get-tuple-element.41), channel_id=1, source_target_pairs={{0,3},{2,5},{3,7},{1,1},{4,2},{6,4},{7,6},{5,0},{8,11},{10,13},{11... | collective-permute-start | bytes 221192 | tf_op jit(solution)/shard_map/cond/branch_2_fun/ppermute | solution.py:283
  (58 other events, 139.1 us)
